TPU v7x, 128 devices: a whole 4x4x4 slice. The times are simulated.
128 devices in a mesh: rel: 4 (over z), ent: 32 (over y, x, core).
Axes of the slice: x: 4, y: 4, z: 4, core: 2. Of those that a mesh axis runs over, the one named last changes fastest.
Arguments:
- features: bfloat16 [16384, 512], P('ent'), may hold values from -6 to 6
- w_self: bfloat16 [512, 512], replicated, may hold values from -0.25 to 0.25
- basis_mats: bfloat16 [16384, 512], replicated, may hold values from -0.046875 to 0.046875
- basis_coeffs: float32 [1000, 32], replicated, may hold values from -5 to 5
- group_rels: int32 [1000], P('rel'), may hold values from 0 to 999, each once
- rel_local: int32 [65536], P(('rel', 'ent')), may hold values from 0 to 249
- edge_src: int32 [65536], P(('rel', 'ent')), may hold values from 0 to 16383, as said below
- edge_dst: int32 [65536], P(('rel', 'ent')), may hold values from 0 to 16383, as said below
- block_counts: int32 [4, 32, 32], P('rel', 'ent'), may hold values from 1 to 16, as said below
- cotangent: bfloat16 [16384, 512], P('ent'), may hold values from -6 to 6
Outputs:
- activations: bfloat16 [16384, 512], P('ent')
- grad_features: bfloat16 [16384, 512], P('ent')
- grad_basis: float32 [16384, 512], P(('rel', 'ent'))
Inputs may be any that keep to these rules, and one draw needn't show every extreme that they name: `edge_src`: slot i's source is owned by ent index (i // 512) % 32: it lies in [that index * 512, that index * 512 + 512). `edge_dst`: slot i's destination is owned by block index k = (i % 512) // 16: it lies in [k * 512, k * 512 + 512); within each aligned block of 16 slots the destinations are non-decreasing; the live slots of a block are its first block_counts ones. `block_counts`: one relation group, drawn from the seed, has every block full.
All inputs are finite; a program needn't handle non-finite values.
Results may differ from a plain program's by a relative error of at most 0.0059.
Values may be sent and summed in bfloat16 or wider, within the bound.
A program may use at most 192 MiB of HBM per device.

v0:
```python
import jax
import jax.numpy as jnp
from jax import lax
from jax.sharding import PartitionSpec as P


def activate(features, w_self, partial_sums, in_degree, cotangent):
    inverse = 1.0 / jnp.maximum(in_degree, 1.0)
    pre_act = (
        jnp.dot(features, w_self, preferred_element_type=jnp.float32)
        + partial_sums * inverse[:, None]
    )
    sigmoid_pre = jax.nn.sigmoid(pre_act)
    out_rows = (pre_act * sigmoid_pre).astype(jnp.bfloat16)
    grad_pre = (
        cotangent.astype(jnp.float32) * (sigmoid_pre * (1.0 + pre_act * (1.0 - sigmoid_pre)))
    ).astype(jnp.bfloat16)
    grad_scaled = (grad_pre.astype(jnp.float32) * inverse[:, None]).astype(jnp.bfloat16)
    return (out_rows, grad_pre, grad_scaled)


def per_device(
    features,
    w_self,
    basis_mats,
    basis_coeffs,
    group_rels,
    rel_local,
    edge_src,
    edge_dst,
    block_counts,
    cotangent,
):
    ent_dev, feat_width = features.shape
    ent_count = lax.axis_size("ent")
    slot_count = rel_local.shape[0]
    block_cap = slot_count // ent_count
    basis_count = basis_coeffs.shape[1]
    first_row = lax.axis_index("ent") * ent_dev
    slot_index = jnp.arange(slot_count, dtype=jnp.int32)
    limits = jnp.repeat(block_counts.reshape(ent_count), block_cap, total_repeat_length=slot_count)
    is_live = slot_index % block_cap < limits
    rel_coef = basis_coeffs[group_rels[rel_local]]
    src_local = edge_src - first_row
    src_rows = features[src_local].astype(jnp.float32)
    mixed_rows = (
        (rel_coef[:, :, None] * src_rows[:, None, :])
        .reshape(slot_count, basis_count * feat_width)
        .astype(jnp.bfloat16)
    )
    product = jnp.dot(mixed_rows, basis_mats, preferred_element_type=jnp.float32)
    messages = (product * is_live.astype(jnp.float32)[:, None]).astype(jnp.bfloat16)
    owner_base = slot_index // block_cap * ent_dev
    targets = jnp.where(is_live, edge_dst - owner_base, ent_dev)
    arrived, dest_slots = (
        lax.all_to_all(
            messages.reshape(ent_count, block_cap, feat_width),
            "ent",
            split_axis=0,
            concat_axis=0,
            tiled=True,
        ),
        lax.all_to_all(
            targets.reshape(ent_count, block_cap), "ent", split_axis=0, concat_axis=0, tiled=True
        ),
    )
    arrived = arrived.reshape(slot_count, feat_width)
    dest_slots = dest_slots.reshape(slot_count)
    one_hot = (dest_slots[None, :] == jnp.arange(ent_dev, dtype=jnp.int32)[:, None]).astype(
        jnp.bfloat16
    )
    partial_sums = jnp.dot(one_hot, arrived, preferred_element_type=jnp.float32)
    in_degree = jnp.sum(one_hot, axis=1, dtype=jnp.float32)
    partial_sums, in_degree = lax.psum((partial_sums, in_degree), "rel")
    out_rows, grad_pre, grad_scaled = activate(features, w_self, partial_sums, in_degree, cotangent)
    picked = grad_scaled[jnp.minimum(dest_slots, ent_dev - 1)]
    grad_back = jnp.where((dest_slots < ent_dev)[:, None], picked, jnp.zeros((), jnp.bfloat16))
    returned = lax.all_to_all(
        grad_back.reshape(ent_count, block_cap, feat_width),
        "ent",
        split_axis=0,
        concat_axis=0,
        tiled=True,
    )
    returned = returned.reshape(slot_count, feat_width)
    grad_mixed = lax.dot_general(
        returned, basis_mats, (((1,), (1,)), ((), ())), preferred_element_type=jnp.float32
    )
    grad_rows = jnp.sum(
        grad_mixed.reshape(slot_count, basis_count, feat_width) * rel_coef[:, :, None], axis=1
    )
    grad_src = jax.ops.segment_sum(grad_rows, src_local, ent_dev)
    grad_src = lax.psum(grad_src, "rel")
    self_part = lax.dot_general(
        grad_pre, w_self, (((1,), (1,)), ((), ())), preferred_element_type=jnp.float32
    )
    grad_features = (self_part + grad_src).astype(jnp.bfloat16)
    grad_basis = lax.psum_scatter(
        lax.dot_general(
            mixed_rows, returned, (((0,), (0,)), ((), ())), preferred_element_type=jnp.float32
        ),
        ("rel", "ent"),
        scatter_dimension=0,
        tiled=True,
    )
    return (out_rows, grad_features, grad_basis)


def solution(mesh):
    placed = (
        P("ent", None),
        P(),
        P(),
        P(),
        P("rel"),
        P(("rel", "ent")),
        P(("rel", "ent")),
        P(("rel", "ent")),
        P("rel", "ent", None),
        P("ent", None),
    )
    return jax.shard_map(
        per_device,
        mesh=mesh,
        in_specs=placed,
        out_specs=(P("ent", None), P("ent", None), P(("rel", "ent"), None)),
        check_vma=False,
    )
```

profile of v0, /device:TPU:0, one launch (start us, length us, event | category | flops | bytes accessed | tf_op | source)
XLA Modules:
  0.0 951.0 jit_solution(16518272372429316720)
XLA Ops:
  7.2 0.0 copy-start
  7.2 1.8 fusion.18
  9.0 2.1 fusion.17
  11.1 0.8 add_add_fusion.1
  11.9 4.5 compare_select_fusion.3
  16.4 0.2 compare_reduce_fusion.24
  16.5 16.4 %fusion.11 = (s32[512]{0:T(512)S(1)}, pred[512]{0:T(512)(128)(4,1)S(1)}) fusion(s32[512]{0:T(512)} %param.19, pred[512]{0:T(512)(128)(4,1)S(1)} %get-tuple-element.41, pred[512]{0:T(512)(128)(4,1)S(1)} %get-tuple-element.40, pred[512]{0:T(512)(128)(4,1)S(1)} %get-tuple-element.39, pred[512]{0:T(512)(128)(4,1)S(1)} %get-tuple-element.38, ...), kind=kLoop, calls=%fused_computation.77 | loop fusion | flops 25600 | bytes 21620 | tf_op jit(solution)/shard_map/jit(_where)/select_n | solution.py:54
  32.9 0.7 all_to_all.12
  33.6 7.4 all-to-all-start
  41.0 0.7 compare_select_fusion.10
  41.7 3.6 gather_fusion
  45.3 0.7 compare_select_fusion.9
  46.0 1.1 copy.29
  47.1 1.0 gather_fusion.1
  48.2 0.1 copy.30
  48.3 2.0 gather_fusion.2
  50.3 0.1 convert_element_type.54
  50.4 6.1 multiply_convert_fusion
  56.5 22.5 %copy.31 = bf16[512,32,512]{0,2,1:T(8,128)(2,1)} copy(bf16[512,32,512]{2,0,1:T(8,128)(2,1)} %multiply_convert_fusion) | data formatting | bytes 33554432 | tf_op jit(solution)/shard_map/convert_element_type | solution.py:49
  79.0 18.1 %fusion.1 = bf16[512,512]{1,0:T(8,128)(2,1)} fusion(bf16[512,16384]{0,1:T(8,128)(2,1)} %bitcast.70, bf16[16384,512]{1,0:T(8,128)(2,1)} %param.14, f32[512]{0:T(512)S(1)} %convert_element_type.57), kind=kOutput, calls=%fused_computation.11 | convolution fusion | flops 8590458880 | bytes 34080768 | tf_op jit(solution)/shard_map/dot_general | solution.py:51
  97.0 7.4 all-to-all-start.1
  104.4 0.0 all-reduce.3.cloned.1.call-start
  104.5 0.5 broadcast.478
  105.0 0.7 minimum_reduce_fusion
  105.7 0.1 eq.17
  105.8 10.4 %all-to-all-done.1 = bf16[32,16,512]{2,1,0:T(8,128)(2,1)S(1)} async-done(((bf16[32,16,512]{2,1,0:T(8,128)(2,1)}), bf16[32,16,512]{2,1,0:T(8,128)(2,1)S(1)}, u32[]{:S(2)}, u32[]{:S(2)}) %all-to-all-start.1) | async-done | bytes 524320 | tf_op jit(solution)/shard_map/all_to_all | solution.py:56
  116.2 1.5 fusion.3
  117.7 0.0 all-reduce.3.cloned.1.call-update
  117.7 0.0 all-reduce.5.cloned.1.call-start
  117.7 0.1 copy.32
  117.8 0.1 copy.33
  117.9 0.1 min.18
  118.0 0.2 convert_reduce_fusion
  118.2 12.0 %psum.22 = f32[512]{0:T(512)S(1)} all-reduce(f32[512]{0:T(512)S(1)} %convert_reduce_fusion), channel_id=1, replica_groups=mesh['rel'=4,'ent'=32] {'rel'}, use_global_device_ids=true, to_apply=%region_2.3 | all-reduce | flops 512 | bytes 4096 | tf_op jit(solution)/shard_map/psum | solution.py:74
  130.2 32.6 %all-reduce.3.cloned.1.call-done = f32[512,512]{1,0:T(8,128)} async-done(((f32[512,512]{1,0:T(8,128)}), f32[512,512]{1,0:T(8,128)}) %all-reduce.3.cloned.1.call-update) | async-done | bytes 1048592 | tf_op jit(solution)/shard_map/psum | solution.py:74
  162.8 2.9 multiply_convert_fusion.1
  165.6 2.0 gather_fusion.3
  167.6 0.1 broadcast_select_fusion
  167.8 18.7 %all_to_all.19 = bf16[32,16,512]{2,1,0:T(8,128)(2,1)S(1)} all-to-all(bf16[32,16,512]{2,1,0:T(8,128)(2,1)S(1)} %broadcast_select_fusion), channel_id=1, replica_groups=mesh['rel'=4,'ent'=32] {'ent'}, dimensions={0} | all-to-all | bytes 1048576 | tf_op jit(solution)/shard_map/all_to_all | solution.py:78
  186.4 12.7 %multiply_reduce_fusion = f32[512,512]{1,0:T(8,128)S(1)} fusion(f32[512,32]{0,1:T(8,128)S(1)} %copy.30, bf16[512,512,1]{1,0,2:T(8,128)(2,1)S(1)} %bitcast.74, bf16[32,512,512]{2,1,0:T(8,128)(2,1)} %bitcast.82), kind=kOutput, calls=%fused_computation.5 | convolution fusion | flops 8606449664 | bytes 18415616 | tf_op jit(solution)/shard_map/dot_general | solution.py:86
  199.1 4.6 scatter_custom_fusion
  203.7 0.0 all-reduce.5.cloned.1.call-update
  203.7 0.3 reduce-scatter.2.cloned.1.call-start
  204.0 21.5 %fusion.19 = f32[16384,512]{1,0:T(8,128)} fusion(bf16[512,16384]{0,1:T(8,128)(2,1)} %bitcast.71, bf16[512,512]{1,0:T(8,128)(2,1)S(1)} %bitcast.75), kind=kOutput, calls=%fused_computation.89 | convolution fusion | flops 8589934592 | bytes 50855936 | tf_op jit(solution)/shard_map/dot_general | solution.py:99
  225.5 0.0 reduce-scatter.2.cloned.1.call-update
  225.5 21.8 %all-reduce.5.cloned.1.call-done = f32[512,512]{1,0:T(8,128)} async-done(((f32[512,512]{1,0:T(8,128)}), f32[512,512]{1,0:T(8,128)}) %all-reduce.5.cloned.1.call-update) | async-done | bytes 1048592 | tf_op jit(solution)/shard_map/psum | solution.py:93
  247.3 2.5 fusion
  249.8 694.7 %reduce-scatter.2.cloned.1.call-done = f32[128,512]{1,0:T(8,128)} async-done(((f32[16384,512]{1,0:T(8,128)}), f32[128,512]{1,0:T(8,128)}) %reduce-scatter.2.cloned.1.call-update) | async-done | bytes 262160 | tf_op jit(solution)/shard_map/reduce_scatter | solution.py:98
  (18 shorter events, 0.1 us)
Async XLA Ops:
  7.2 41.1 %copy-start = (bf16[512,512]{1,0:T(8,128)(2,1)S(1)}, bf16[512,512]{1,0:T(8,128)(2,1)}, u32[]{:S(2)}) copy-start(bf16[512,512]{1,0:T(8,128)(2,1)} %param.12) | copy-start | bytes 1572868
  33.6 63.5 %all-to-all-start = ((s32[32,1,16]{2,1,0:T(1,128)}), s32[32,1,16]{2,1,0:T(1,128)S(1)}, u32[]{:S(2)}, u32[]{:S(2)}) async-start(s32[32,1,16]{2,1,0:T(1,128)} %bitcast.37), calls=%async_computation | async-start | bytes 32768 | tf_op jit(solution)/shard_map/all_to_all | solution.py:63
  79.0 83.8 %copy-start.2 = (bf16[512,512]{1,0:T(8,128)(2,1)S(1)}, bf16[512,512]{1,0:T(8,128)(2,1)}, u32[]{:S(2)}) copy-start(bf16[512,512]{1,0:T(8,128)(2,1)} %param.13) | copy-start | bytes 1572868
  79.0 83.8 %copy-start.3 = (bf16[512,512]{1,0:T(8,128)(2,1)S(1)}, bf16[512,512]{1,0:T(8,128)(2,1)}, u32[]{:S(2)}) copy-start(bf16[512,512]{1,0:T(8,128)(2,1)} %param.21) | copy-start | bytes 1572868
  97.0 19.1 %all-to-all-start.1 = ((bf16[32,16,512]{2,1,0:T(8,128)(2,1)}), bf16[32,16,512]{2,1,0:T(8,128)(2,1)S(1)}, u32[]{:S(2)}, u32[]{:S(2)}) async-start(bf16[32,16,512]{2,1,0:T(8,128)(2,1)} %bitcast.41), calls=%async_computation.1 | async-start | bytes 1048576 | tf_op jit(solution)/shard_map/all_to_all | solution.py:56
  104.4 58.3 %all-reduce.3.cloned.1.call-start = ((), (), s32[]{:S(2)}) async-start(), calls=%async_computation.4 | async-start | bytes 2097152 | tf_op jit(solution)/shard_map/psum | solution.py:74
  117.7 129.6 %all-reduce.5.cloned.1.call-start = ((), (), s32[]{:S(2)}) async-start(), calls=%async_computation.5 | async-start | bytes 2097152 | tf_op jit(solution)/shard_map/psum | solution.py:93
  203.7 740.8 %reduce-scatter.2.cloned.1.call-start = ((), (), s32[]{:S(2)}) async-start(), calls=%async_computation.6 | async-start | bytes 33816576 | tf_op jit(solution)/shard_map/reduce_scatter | solution.py:98
  225.5 719.0 %copy-start.1 = (bf16[512,512]{1,0:T(8,128)(2,1)S(1)}, bf16[512,512]{1,0:T(8,128)(2,1)}, u32[]{:S(2)}) copy-start(bf16[512,512]{1,0:T(8,128)(2,1)} %param.12) | copy-start | bytes 1572868
Sparse Core Ops, SparseCore 0:
  117.8 44.9 all-reduce.2
  203.8 43.4 all-reduce.4
  250.3 694.1 reduce-scatter.1
where the time goes:
time: 952 us; the launch traced here: 951 us
  waiting for transfers between devices  759 us (80%)
  matrix products  59.1 us (6%)
  local copies, waits for them, and re-layouts  37.8 us (4%)
  other arithmetic  35 us (4%)
  blocking collectives  30.7 us (3%)
  starting transfers between devices  15.1 us (2%)
  between operations  13.9 us (1%)
    reduce_scatter x1, waiting for transfers between devices, per_device(): lax.psum_scatter(lax.dot_general(mixed_rows, returned, (((0,), (0,)), (()...  695 us
    psum x1, waiting for transfers between devices, per_device(): partial_sums, in_degree = lax.psum((partial_sums, in_degree), 'rel')  32.6 us
    convert_element_type x1, local copies, waits for them, and re-layouts, per_device(): mixed_rows = (rel_coef[:, :, None] * src_rows[:, None, :]).reshape(slot_c...  22.5 us
    psum x1, waiting for transfers between devices, per_device(): grad_src = lax.psum(grad_src, 'rel')  21.8 us
    dot_general x1, matrix products, per_device(): lax.dot_general(mixed_rows, returned, (((0,), (0,)), ((), ())), preferred...  21.5 us
  transfers between devices with their start and end apart: 5, of which 4 were waited for; matrix products, arithmetic and copies ran while one was open for 9% of the time, Pallas kernels for 0%

commit v1 on v0

--- a/solution.py
+++ b/solution.py
@@ -90,7 +90,9 @@
         grad_mixed.reshape(slot_count, basis_count, feat_width) * rel_coef[:, :, None], axis=1
     )
     grad_src = jax.ops.segment_sum(grad_rows, src_local, ent_dev)
-    grad_src = lax.psum(grad_src, "rel")
+    grad_src = grad_src
+    for hop in (1, 2):
+        grad_src = grad_src + lax.ppermute(grad_src, "rel", [(dev, dev ^ hop) for dev in range(4)])
     self_part = lax.dot_general(
         grad_pre, w_self, (((1,), (1,)), ((), ())), preferred_element_type=jnp.float32
     )

time: 952 us -> 910 us (0.956)
  waiting for transfers between devices: 759 us -> 714 us
    reduce_scatter x1, waiting for transfers between devices: 695 us -> 599 us  [per_device(): lax.psum_scatter(lax.dot_general(mixed_rows, returned, (((0,), (0,)), (()...]
    ppermute x0 -> x2, waiting for transfers between devices: none -> 71 us  [per_device(): lax.ppermute(grad_src, 'rel', [(dev, dev ^ hop) for dev in range(4)])]
    psum x1 -> x0, waiting for transfers between devices: 21.8 us -> none  [per_device(): grad_src = lax.psum(grad_src, 'rel')]
  transfers between devices with their start and end apart: 5 -> 6, of which waited for: 4 -> 5; matrix products, arithmetic and copies ran while one was open for 9% -> 9% of each run, Pallas kernels for 0% -> 0%
where the time goes in v1:
time: 910 us; the launch traced here: 909 us
  waiting for transfers between devices  714 us (78%)
  matrix products  58.2 us (6%)
  local copies, waits for them, and re-layouts  37.8 us (4%)
  other arithmetic  36.2 us (4%)
  blocking collectives  30.5 us (3%)
  starting transfers between devices  18.2 us (2%)
  between operations  14.2 us (2%)
    reduce_scatter x1, waiting for transfers between devices, per_device(): lax.psum_scatter(lax.dot_general(mixed_rows, returned, (((0,), (0,)), (()...  599 us
    ppermute x2, waiting for transfers between devices, per_device(): lax.ppermute(grad_src, 'rel', [(dev, dev ^ hop) for dev in range(4)])  71 us
    psum x1, waiting for transfers between devices, per_device(): partial_sums, in_degree = lax.psum((partial_sums, in_degree), 'rel')  32.8 us
    convert_element_type x1, local copies, waits for them, and re-layouts, per_device(): mixed_rows = (rel_coef[:, :, None] * src_rows[:, None, :]).reshape(slot_c...  22.5 us
    dot_general x1, matrix products, per_device(): lax.dot_general(mixed_rows, returned, (((0,), (0,)), ((), ())), preferred...  21.2 us
    all_to_all x1, blocking collectives, per_device(): lax.all_to_all(grad_back.reshape(ent_count, block_cap, feat_width), 'ent'...  18.7 us
  transfers between devices with their start and end apart: 6, of which 5 were waited for; matrix products, arithmetic and copies ran while one was open for 9% of the time, Pallas kernels for 0%

profile of v1, /device:TPU:0, one launch (start us, length us, event | category | flops | bytes accessed | tf_op | source)
XLA Modules:
  0.0 908.5 jit_solution(12462984252919640551)
XLA Ops:
  7.2 1.8 fusion.17
  9.0 2.1 fusion.16
  11.1 0.8 add_add_fusion.1
  11.9 4.5 compare_select_fusion.3
  16.4 0.2 compare_reduce_fusion.24
  16.5 16.4 %fusion.10 = (s32[512]{0:T(512)S(1)}, pred[512]{0:T(512)(128)(4,1)S(1)}) fusion(s32[512]{0:T(512)} %param.19, pred[512]{0:T(512)(128)(4,1)S(1)} %get-tuple-element.41, pred[512]{0:T(512)(128)(4,1)S(1)} %get-tuple-element.40, pred[512]{0:T(512)(128)(4,1)S(1)} %get-tuple-element.39, pred[512]{0:T(512)(128)(4,1)S(1)} %get-tuple-element.38, ...), kind=kLoop, calls=%fused_computation.76 | loop fusion | flops 25600 | bytes 21620 | tf_op jit(solution)/shard_map/jit(_where)/select_n | solution.py:54
  32.9 0.7 all_to_all.12
  33.6 7.4 all-to-all-start
  41.0 0.7 compare_select_fusion.10
  41.7 3.6 gather_fusion
  45.3 0.7 compare_select_fusion.9
  46.0 1.1 copy.29
  47.1 1.0 gather_fusion.1
  48.2 0.1 copy.30
  48.3 2.0 gather_fusion.2
  50.3 0.1 convert_element_type.54
  50.4 6.1 multiply_convert_fusion
  56.5 22.5 %copy.31 = bf16[512,32,512]{0,2,1:T(8,128)(2,1)} copy(bf16[512,32,512]{2,0,1:T(8,128)(2,1)} %multiply_convert_fusion) | data formatting | bytes 33554432 | tf_op jit(solution)/shard_map/convert_element_type | solution.py:49
  79.0 18.1 %fusion = bf16[512,512]{1,0:T(8,128)(2,1)} fusion(bf16[512,16384]{0,1:T(8,128)(2,1)} %bitcast.70, bf16[16384,512]{1,0:T(8,128)(2,1)} %param.14, f32[512]{0:T(512)S(1)} %convert_element_type.57), kind=kOutput, calls=%fused_computation.9 | convolution fusion | flops 8590458880 | bytes 34080768 | tf_op jit(solution)/shard_map/dot_general | solution.py:51
  97.0 7.4 all-to-all-start.1
  104.4 0.0 all-reduce.2.cloned.1.call-start
  104.5 0.5 broadcast.478
  105.0 0.7 minimum_reduce_fusion
  105.7 0.1 eq.17
  105.8 10.4 %all-to-all-done.1 = bf16[32,16,512]{2,1,0:T(8,128)(2,1)S(1)} async-done(((bf16[32,16,512]{2,1,0:T(8,128)(2,1)}), bf16[32,16,512]{2,1,0:T(8,128)(2,1)S(1)}, u32[]{:S(2)}, u32[]{:S(2)}) %all-to-all-start.1) | async-done | bytes 524320 | tf_op jit(solution)/shard_map/all_to_all | solution.py:56
  116.2 1.5 fusion.2
  117.7 0.0 reduce-scatter.2.cloned.1.call-start
  117.7 0.1 copy.32
  117.8 0.1 copy.33
  117.9 0.1 min.18
  118.0 0.2 convert_reduce_fusion
  118.2 11.8 %psum.15 = f32[512]{0:T(512)S(1)} all-reduce(f32[512]{0:T(512)S(1)} %convert_reduce_fusion), channel_id=1, replica_groups=mesh['rel'=4,'ent'=32] {'rel'}, use_global_device_ids=true, to_apply=%region_2.3 | all-reduce | flops 512 | bytes 4096 | tf_op jit(solution)/shard_map/psum | solution.py:74
  130.0 32.8 %all-reduce.2.cloned.1.call-done = f32[512,512]{1,0:T(8,128)} async-done(((f32[512,512]{1,0:T(8,128)}), f32[512,512]{1,0:T(8,128)}) %all-reduce.2.cloned.1.call-update) | async-done | bytes 1048592 | tf_op jit(solution)/shard_map/psum | solution.py:74
  162.8 2.9 multiply_convert_fusion.1
  165.6 2.0 gather_fusion.3
  167.6 0.1 broadcast_select_fusion
  167.8 18.7 %all_to_all.19 = bf16[32,16,512]{2,1,0:T(8,128)(2,1)S(1)} all-to-all(bf16[32,16,512]{2,1,0:T(8,128)(2,1)S(1)} %broadcast_select_fusion), channel_id=1, replica_groups=mesh['rel'=4,'ent'=32] {'ent'}, dimensions={0} | all-to-all | bytes 1048576 | tf_op jit(solution)/shard_map/all_to_all | solution.py:78
  186.4 21.2 %fusion.19 = f32[16384,512]{1,0:T(8,128)} fusion(bf16[512,16384]{0,1:T(8,128)(2,1)} %bitcast.71, bf16[512,512]{1,0:T(8,128)(2,1)S(1)} %bitcast.74), kind=kOutput, calls=%fused_computation.89 | convolution fusion | flops 8589934592 | bytes 50855936 | tf_op jit(solution)/shard_map/dot_general | solution.py:101
  207.7 14.1 %multiply_reduce_fusion = f32[512,512]{1,0:T(8,128)} fusion(f32[512,32]{0,1:T(8,128)S(1)} %copy.30, bf16[512,512,1]{1,0,2:T(8,128)(2,1)S(1)} %bitcast.75, bf16[32,512,512]{2,1,0:T(8,128)(2,1)} %bitcast.82), kind=kOutput, calls=%fused_computation.5 | convolution fusion | flops 8606449664 | bytes 18415616 | tf_op jit(solution)/shard_map/dot_general | solution.py:86
  221.8 4.5 scatter_custom_fusion
  226.3 0.6 collective-permute-start
  226.8 32.5 %collective-permute-done = f32[512,512]{1,0:T(8,128)S(1)} collective-permute-done((f32[512,512]{1,0:T(8,128)S(1)}, f32[512,512]{1,0:T(8,128)S(1)}, u32[]{:S(2)}, u32[]{:S(2)}) %collective-permute-start) | collective-permute-done | bytes 1048608 | tf_op jit(solution)/shard_map/ppermute | solution.py:95
  259.3 0.2 add.141
  259.5 2.8 collective-permute-start.1
  262.3 0.5 fusion.18
  262.7 38.6 %collective-permute-done.1 = f32[512,512]{1,0:T(8,128)S(1)} collective-permute-done((f32[512,512]{1,0:T(8,128)S(1)}, f32[512,512]{1,0:T(8,128)S(1)}, u32[]{:S(2)}, u32[]{:S(2)}) %collective-permute-start.1) | collective-permute-done | bytes 1048608 | tf_op jit(solution)/shard_map/ppermute | solution.py:95
  301.3 1.1 add_convert_fusion
  302.4 599.3 %reduce-scatter.2.cloned.1.call-done = f32[128,512]{1,0:T(8,128)} async-done(((f32[16384,512]{1,0:T(8,128)}), f32[128,512]{1,0:T(8,128)}) %reduce-scatter.2.cloned.1.call-update) | async-done | bytes 262160 | tf_op jit(solution)/shard_map/reduce_scatter | solution.py:100
  (21 shorter events, 0.1 us)
Async XLA Ops:
  7.2 41.1 %copy-start = (bf16[512,512]{1,0:T(8,128)(2,1)S(1)}, bf16[512,512]{1,0:T(8,128)(2,1)}, u32[]{:S(2)}) copy-start(bf16[512,512]{1,0:T(8,128)(2,1)} %param.12) | copy-start | bytes 1572868
  33.6 63.5 %all-to-all-start = ((s32[32,1,16]{2,1,0:T(1,128)}), s32[32,1,16]{2,1,0:T(1,128)S(1)}, u32[]{:S(2)}, u32[]{:S(2)}) async-start(s32[32,1,16]{2,1,0:T(1,128)} %bitcast.37), calls=%async_computation | async-start | bytes 32768 | tf_op jit(solution)/shard_map/all_to_all | solution.py:63
  79.0 83.8 %copy-start.2 = (bf16[512,512]{1,0:T(8,128)(2,1)S(1)}, bf16[512,512]{1,0:T(8,128)(2,1)}, u32[]{:S(2)}) copy-start(bf16[512,512]{1,0:T(8,128)(2,1)} %param.13) | copy-start | bytes 1572868
  79.0 83.8 %copy-start.3 = (bf16[512,512]{1,0:T(8,128)(2,1)S(1)}, bf16[512,512]{1,0:T(8,128)(2,1)}, u32[]{:S(2)}) copy-start(bf16[512,512]{1,0:T(8,128)(2,1)} %param.21) | copy-start | bytes 1572868
  97.0 19.1 %all-to-all-start.1 = ((bf16[32,16,512]{2,1,0:T(8,128)(2,1)}), bf16[32,16,512]{2,1,0:T(8,128)(2,1)S(1)}, u32[]{:S(2)}, u32[]{:S(2)}) async-start(bf16[32,16,512]{2,1,0:T(8,128)(2,1)} %bitcast.41), calls=%async_computation.1 | async-start | bytes 1048576 | tf_op jit(solution)/shard_map/all_to_all | solution.py:56
  104.4 58.3 %all-reduce.2.cloned.1.call-start = ((), (), s32[]{:S(2)}) async-start(), calls=%async_computation.4 | async-start | bytes 2097152 | tf_op jit(solution)/shard_map/psum | solution.py:74
  117.7 784.0 %reduce-scatter.2.cloned.1.call-start = ((), (), s32[]{:S(2)}) async-start(), calls=%async_computation.5 | async-start | bytes 33816576 | tf_op jit(solution)/shard_map/reduce_scatter | solution.py:100
  207.7 694.0 %copy-start.1 = (bf16[512,512]{1,0:T(8,128)(2,1)S(1)}, bf16[512,512]{1,0:T(8,128)(2,1)}, u32[]{:S(2)}) copy-start(bf16[512,512]{1,0:T(8,128)(2,1)} %param.12) | copy-start | bytes 1572868
  226.3 33.0 %collective-permute-start = (f32[512,512]{1,0:T(8,128)S(1)}, f32[512,512]{1,0:T(8,128)S(1)}, u32[]{:S(2)}, u32[]{:S(2)}) collective-permute-start(f32[512,512]{1,0:T(8,128)S(1)} %scatter_custom_fusion), channel_id=1, source_target_pairs={{0,32},{32,0},{64,96},{96,64},{1,33},{33,1},{65,97},{97,65},{2,34}... | collective-permute-start | bytes 3145736 | tf_op jit(solution)/shard_map/ppermute | solution.py:95
  259.5 41.8 %collective-permute-start.1 = (f32[512,512]{1,0:T(8,128)S(1)}, f32[512,512]{1,0:T(8,128)S(1)}, u32[]{:S(2)}, u32[]{:S(2)}) collective-permute-start(f32[512,512]{1,0:T(8,128)S(1)} %add.141), channel_id=1, source_target_pairs={{0,64},{32,96},{64,0},{96,32},{1,65},{33,97},{65,1},{97,33},{2,66}... | collective-permute-start | bytes 3145736 | tf_op jit(solution)/shard_map/ppermute | solution.py:95
Sparse Core Ops, SparseCore 0:
  117.8 44.9 all-reduce.1
  207.8 693.8 reduce-scatter.1
